TPU v7x, 512 devices: a whole 4x4x16 slice. The times are simulated.
512 devices in a mesh: occ: 64 (over y, z), vir: 8 (over x, core).
Axes of the slice: x: 4, y: 4, z: 16, core: 2. Of those that a mesh axis runs over, the one named last changes fastest.
Arguments:
- t2_tiles: bfloat16 [16384, 128, 128], P(('occ', 'vir')), may hold values from -6 to 6
- tile_owner: int32 [16384, 1], P(('occ', 'vir')), may hold values from 0 to 63; in each aligned block of 32 rows (0 to 31, 32 to 63, ...) at most 2 rows name the same one
- tile_block: int32 [16384], P(('occ', 'vir')), may hold values from 0 to 1
- tile_cd: int32 [16384], P(('occ', 'vir')), may hold values from 0 to 3
- ladder_ints: bfloat16 [4096, 2048], P('vir', 'occ'), may hold values from -0.75 to 0.75
- cycle_amps: bfloat16 [16384, 1024], P('occ', 'vir'), may hold values from -6 to 6
- cycle_ints: bfloat16 [1024, 2048], P('vir'), may hold values from -0.25 to 0.25
Outputs:
- residual: bfloat16 [16384, 2048], P('occ', 'vir')
Inputs may be any that keep to these rules, and one draw needn't show every extreme that they name: `tile_owner`: among the tiles of one device (aligned blocks of 32 tiles), no owner is named more than 2 times, a bound that some block reaches.
All inputs are finite; a program needn't handle non-finite values.
Results may differ from a plain program's by a relative error of at most 0.0048.
Values may be sent and summed in bfloat16 or wider, within the bound.
A program may use at most 64 MiB of HBM per device.

v0:
```python
import jax
import jax.numpy as jnp
from jax import lax
from jax.sharding import PartitionSpec as P

NY = 4


def body(t2_tiles, tile_owner, tile_block, tile_cd, ladder_ints, cycle_amps, cycle_ints):
    n_occ = lax.axis_size("occ")
    nz = n_occ // NY
    tile_count, tile_size = t2_tiles.shape[:2]
    pair_rows = cycle_amps.shape[0]
    blocks = pair_rows // tile_size
    cd_tiles = ladder_ints.shape[0] // tile_size
    combos = blocks * cd_tiles
    y_groups = [[y * nz + z for y in range(NY)] for z in range(nz)]
    z_groups = [[y * nz + z for z in range(nz)] for y in range(NY)]
    codes = tile_owner[:, 0] * combos + tile_block * cd_tiles + tile_cd
    got_tiles = lax.all_gather(
        t2_tiles.reshape(tile_count, tile_size * tile_size),
        "occ",
        axis=0,
        tiled=True,
        axis_index_groups=y_groups,
    )
    got_codes = lax.all_gather(codes, "occ", axis=0, tiled=True, axis_index_groups=y_groups)
    full_ladder = lax.all_gather(ladder_ints, "occ", axis=1, tiled=True)
    my_y = lax.axis_index("occ") // nz
    targets = my_y * (nz * combos) + jnp.arange(nz * combos, dtype=jnp.int32)
    select = (got_codes[:, None] == targets[None, :]).astype(jnp.bfloat16)
    summed = jnp.einsum("sc,sx->cx", select, got_tiles, preferred_element_type=jnp.float32)
    summed = lax.psum_scatter(
        summed.astype(jnp.bfloat16),
        "occ",
        scatter_dimension=0,
        tiled=True,
        axis_index_groups=z_groups,
    )
    amplitudes = (
        summed.reshape(blocks, cd_tiles, tile_size, tile_size)
        .transpose(0, 2, 1, 3)
        .reshape(pair_rows, cd_tiles * tile_size)
    )
    cycle_part = jnp.dot(cycle_amps, cycle_ints, preferred_element_type=jnp.float32)
    ladder = jnp.dot(amplitudes, full_ladder, preferred_element_type=jnp.float32)
    combined = ladder + cycle_part
    return lax.psum_scatter(combined, "vir", scatter_dimension=1, tiled=True).astype(jnp.bfloat16)


def solution(mesh):
    in_specs = (
        P(("occ", "vir"), None, None),
        P(("occ", "vir"), None),
        P(("occ", "vir")),
        P(("occ", "vir")),
        P("vir", "occ"),
        P("occ", "vir"),
        P("vir", None),
    )
    return jax.shard_map(
        body, mesh=mesh, in_specs=in_specs, out_specs=P("occ", "vir"), check_vma=False
    )
```

profile of v0, /device:TPU:8, one launch (start us, length us, event | category | flops | bytes accessed | tf_op | source)
XLA Modules:
  0.0 276.3 jit_solution(14078321033203667457)
XLA Ops:
  7.4 0.0 copy-start
  7.4 0.0 copy-start.2
  7.4 0.0 copy-start.4
  7.4 0.0 copy-start.3
  7.4 0.0 all-gather.3.cloned.1.call-start
  7.4 2.9 %copy.17 = bf16[4,8,128,128]{3,1,2,0:T(8,128)(2,1)} copy(bf16[4,8,128,128]{3,2,1,0:T(8,128)(2,1)} %bitcast.26) | data formatting | bytes 2097152
  10.3 0.0 all-gather.3.cloned.1.call-update
  10.4 0.0 reduce-scatter.3.cloned.1.call-start
  10.4 1.3 dynamic-slice
  12.4 0.0 copy-done.2
  12.4 0.0 copy-done.4
  12.4 0.0 copy-done.3
  12.4 0.1 fusion.6
  12.5 9.4 %all-reduce = s32[128]{0:T(128)S(1)} all-reduce(s32[128]{0:T(128)S(1)} %fusion.6), channel_id=1, replica_groups={{0,128,256,384},{8,136,264,392},{16,144,272,400},{24,152,280,408},{32,1..., use_global_device_ids=true, to_apply=%add | all-reduce | flops 128 | bytes 1024
  21.9 48.3 %all-gather.3.cloned.1.call-done = bf16[128,16384]{1,0:T(8,128)(2,1)} async-done(((bf16[32,16384]{1,0:T(8,128)(2,1)}), bf16[128,16384]{1,0:T(8,128)(2,1)}) %all-gather.3.cloned.1.call-update) | async-done | bytes 4194320 | tf_op jit(solution)/shard_map/all_gather | solution.py:20
  70.2 5.5 %convolution_convert_fusion = bf16[128,16384]{1,0:T(8,128)(2,1)} fusion(bf16[128,16384]{1,0:T(8,128)(2,1)} %all-gather.3.cloned.1.call-done, s32[128]{0:T(128)S(1)} %iota_add_fusion, s32[128]{0:T(128)S(1)} %all-reduce), kind=kOutput, calls=%fused_computation | convolution fusion | flops 538984448 | bytes 8389632 | tf_op jit(solution)/shard_map/sc,sx->cx/dot_general | solution.py:32
  75.7 0.0 copy-start.1
  75.7 0.0 reduce-scatter.3.cloned.1.call-update
  75.7 0.0 all-gather.5.cloned.1.call-start
  75.8 0.5 all-gather.5.cloned.1.call-update
  76.3 0.0 reduce-scatter.5.cloned.1.call-start
  76.4 0.0 copy-done
  76.4 0.2 copy-done.1
  76.5 0.4 fusion.7
  77.0 79.8 %reduce-scatter.3.cloned.1.call-done = bf16[8,16384]{1,0:T(8,128)(2,1)} async-done(((bf16[128,16384]{1,0:T(8,128)(2,1)}), bf16[8,16384]{1,0:T(8,128)(2,1)}) %reduce-scatter.3.cloned.1.call-update) | async-done | bytes 262160 | tf_op jit(solution)/shard_map/reduce_scatter | solution.py:33
  156.7 1.0 copy.10
  157.7 0.2 copy.8
  157.9 67.5 %all-gather.5.cloned.1.call-done = bf16[512,2048]{0,1:T(8,128)(2,1)} async-done(((bf16[512,32]{0,1:T(8,128)(2,1)}), bf16[512,2048]{0,1:T(8,128)(2,1)}) %all-gather.5.cloned.1.call-update) | async-done | bytes 2097168 | tf_op jit(solution)/shard_map/all_gather | solution.py:28
  225.4 3.7 %convolution_add_fusion = f32[256,2048]{1,0:T(8,128)} fusion(f32[256,2048]{1,0:T(8,128)S(1)} %fusion.7, bf16[512,2048]{0,1:T(8,128)(2,1)} %all-gather.5.cloned.1.call-done, bf16[32,8,4,128]{3,2,1,0:T(4,128)(2,1)S(1)} %bitcast.25), kind=kOutput, calls=%fused_computation.1 | convolution fusion | flops 537395200 | bytes 6553600 | tf_op jit(solution)/shard_map/dot_general | solution.py:46
  229.1 0.0 reduce-scatter.5.cloned.1.call-update
  229.1 38.2 %reduce-scatter.5.cloned.1.call-done = f32[256,256]{1,0:T(8,128)} async-done(((f32[256,2048]{1,0:T(8,128)}), f32[256,256]{1,0:T(8,128)}) %reduce-scatter.5.cloned.1.call-update) | async-done | bytes 262160 | tf_op jit(solution)/shard_map/reduce_scatter | solution.py:48
  267.3 1.6 convert_element_type.8
  (2 shorter events, 0.0 us)
Async XLA Ops:
  7.4 69.0 %copy-start = (bf16[128,2048]{1,0:T(8,128)(2,1)S(1)}, bf16[128,2048]{1,0:T(8,128)(2,1)}, u32[]{:S(2)}) copy-start(bf16[128,2048]{1,0:T(8,128)(2,1)} %param.13) | copy-start | bytes 1572868
  7.4 5.0 %copy-start.2 = (s32[32]{0:T(128)S(1)}, s32[32]{0:T(128)}, u32[]{:S(2)}) copy-start(s32[32]{0:T(128)} %param.10) | copy-start | bytes 388
  7.4 5.0 %copy-start.4 = (s32[32,1]{0,1:T(1,128)S(1)}, s32[32,1]{0,1:T(1,128)}, u32[]{:S(2)}) copy-start(s32[32,1]{0,1:T(1,128)} %param.8) | copy-start | bytes 388
  7.4 5.0 %copy-start.3 = (s32[32]{0:T(128)S(1)}, s32[32]{0:T(128)}, u32[]{:S(2)}) copy-start(s32[32]{0:T(128)} %param.9) | copy-start | bytes 388
  7.4 62.8 %all-gather.3.cloned.1.call-start = ((), (), s32[]{:S(2)}) async-start(), calls=%async_computation.2 | async-start | bytes 5242880 | tf_op jit(solution)/shard_map/all_gather | solution.py:20
  10.4 146.4 %reduce-scatter.3.cloned.1.call-start = ((), (), s32[]{:S(2)}) async-start(), calls=%async_computation.3 | async-start | bytes 4456448 | tf_op jit(solution)/shard_map/reduce_scatter | solution.py:33
  75.7 0.8 copy-start.1
  75.7 149.7 %all-gather.5.cloned.1.call-start = ((), (), s32[]{:S(2)}) async-start(), calls=%async_computation.4 | async-start | bytes 2129920 | tf_op jit(solution)/shard_map/all_gather | solution.py:28
  76.3 191.0 %reduce-scatter.5.cloned.1.call-start = ((), (), s32[]{:S(2)}) async-start(), calls=%async_computation.5 | async-start | bytes 2359296 | tf_op jit(solution)/shard_map/reduce_scatter | solution.py:48
Sparse Core Ops, SparseCore 0:
  10.5 59.6 all-gather.2
  75.8 80.8 reduce-scatter.2
Sparse Core Ops, SparseCore 1:
  79.1 146.2 all-gather.4
  229.2 38.0 reduce-scatter.4
where the time goes:
time: 277 us; the launch traced here: 276 us
  waiting for transfers between devices  234 us (84%)
  between operations  15.6 us (6%)
  matrix products  9.58 us (3%)
  blocking collectives  9.41 us (3%)
  local copies, waits for them, and re-layouts  5.58 us (2%)
    reduce_scatter x1, waiting for transfers between devices, body(): lax.psum_scatter(summed.astype(jnp.bfloat16), 'occ', scatter_dimension=0,...  79.8 us
    all_gather x1, waiting for transfers between devices, body(): full_ladder = lax.all_gather(ladder_ints, 'occ', axis=1, tiled=True)  67.5 us
    all_gather x1, waiting for transfers between devices, body(): lax.all_gather(t2_tiles.reshape(tile_count, tile_size * tile_size), 'occ'...  48.3 us
    reduce_scatter x1, waiting for transfers between devices, body(): lax.psum_scatter(combined, 'vir', scatter_dimension=1, tiled=True)  38.2 us
    unnamed x1, blocking collectives  9.41 us
  transfers between devices with their start and end apart: 4, of which 4 were waited for; matrix products, arithmetic and copies ran while one was open for 1% of the time, Pallas kernels for 0%

commit v1 on v0

--- a/solution.py
+++ b/solution.py
@@ -25,7 +25,9 @@
         axis_index_groups=y_groups,
     )
     got_codes = lax.all_gather(codes, "occ", axis=0, tiled=True, axis_index_groups=y_groups)
-    full_ladder = lax.all_gather(ladder_ints, "occ", axis=1, tiled=True)
+    full_ladder = jnp.concatenate(
+        lax.all_to_all(jnp.stack([ladder_ints] * lax.axis_size("occ")), "occ", 0, 0), axis=1
+    )
     my_y = lax.axis_index("occ") // nz
     targets = my_y * (nz * combos) + jnp.arange(nz * combos, dtype=jnp.int32)
     select = (got_codes[:, None] == targets[None, :]).astype(jnp.bfloat16)

time: 277 us -> 290 us (1.047)
  starting transfers between devices: 0.16 us -> 15.7 us
  waiting for transfers between devices: 234 us -> 231 us
    all_gather x1 -> x0, waiting for transfers between devices: 67.5 us -> none  [body(): full_ladder = lax.all_gather(ladder_ints, 'occ', axis=1, tiled=True)]
    reduce_scatter x1, waiting for transfers between devices: 79.8 us -> 142 us  [body(): lax.psum_scatter(summed.astype(jnp.bfloat16), 'occ', scatter_dimension=0,...]
    all_to_all x0 -> x1, starting transfers between devices: none -> 15.6 us  [body(): lax.all_to_all(jnp.stack([ladder_ints] * lax.axis_size('occ')), 'occ', 0, 0)]
    unnamed x14 -> x16, local copies, waits for them, and re-layouts: 5.37 us -> 5.93 us
  transfers between devices with their start and end apart: 4 -> 4, of which waited for: 4 -> 3; matrix products, arithmetic and copies ran while one was open for 1% -> 2% of each run, Pallas kernels for 0% -> 0%
where the time goes in v1:
time: 290 us
  waiting for transfers between devices  231 us (80%)
  starting transfers between devices  15.7 us (5%)
  between operations  13.9 us (5%)
  matrix products  10.9 us (4%)
  blocking collectives  9.41 us (3%)
  local copies, waits for them, and re-layouts  7.74 us (3%)
    reduce_scatter x1, waiting for transfers between devices, body(): lax.psum_scatter(summed.astype(jnp.bfloat16), 'occ', scatter_dimension=0,...  142 us
    all_gather x1, waiting for transfers between devices, body(): lax.all_gather(t2_tiles.reshape(tile_count, tile_size * tile_size), 'occ'...  48.3 us
    reduce_scatter x1, waiting for transfers between devices, body(): lax.psum_scatter(combined, 'vir', scatter_dimension=1, tiled=True)  40.6 us
    all_to_all x1, starting transfers between devices, body(): lax.all_to_all(jnp.stack([ladder_ints] * lax.axis_size('occ')), 'occ', 0, 0)  15.6 us
    unnamed x1, blocking collectives  9.41 us
    unnamed x16, local copies, waits for them, and re-layouts  5.93 us
  transfers between devices with their start and end apart: 4, of which 3 were waited for; matrix products, arithmetic and copies ran while one was open for 2% of the time, Pallas kernels for 0%

profile of v1, /device:TPU:8, one launch (start us, length us, event | category | flops | bytes accessed | tf_op | source)
XLA Modules:
  0.0 289.9 jit_solution(11249092823229394430)
XLA Ops:
  6.5 0.0 copy-start
  6.5 0.0 copy-start.3
  6.5 0.0 copy-start.4
  6.5 0.0 all-gather.2.cloned.1.call-start
  6.6 2.9 %copy.18 = bf16[4,8,128,128]{3,1,2,0:T(8,128)(2,1)} copy(bf16[4,8,128,128]{3,2,1,0:T(8,128)(2,1)} %bitcast.30) | data formatting | bytes 2097152
  9.5 0.0 all-gather.2.cloned.1.call-update
  9.5 0.0 reduce-scatter.3.cloned.1.call-start
  9.6 1.3 dynamic-slice
  11.5 0.0 copy-done.3
  11.5 0.0 copy-done.4
  11.5 0.0 copy-done.5
  11.6 0.1 fusion.6
  11.7 9.4 %all-reduce = s32[128]{0:T(128)S(1)} all-reduce(s32[128]{0:T(128)S(1)} %fusion.6), channel_id=1, replica_groups={{0,128,256,384},{8,136,264,392},{16,144,272,400},{24,152,280,408},{32,1..., use_global_device_ids=true, to_apply=%add | all-reduce | flops 128 | bytes 1024
  21.1 48.3 %all-gather.2.cloned.1.call-done = bf16[128,16384]{1,0:T(8,128)(2,1)} async-done(((bf16[32,16384]{1,0:T(8,128)(2,1)}), bf16[128,16384]{1,0:T(8,128)(2,1)}) %all-gather.2.cloned.1.call-update) | async-done | bytes 4194320 | tf_op jit(solution)/shard_map/all_gather | solution.py:20
  69.4 5.5 %convolution_convert_fusion = bf16[128,16384]{1,0:T(8,128)(2,1)} fusion(bf16[128,16384]{1,0:T(8,128)(2,1)} %all-gather.2.cloned.1.call-done, s32[128]{0:T(128)S(1)} %iota_add_fusion, s32[128]{0:T(128)S(1)} %all-reduce), kind=kOutput, calls=%fused_computation | convolution fusion | flops 538984448 | bytes 8389632 | tf_op jit(solution)/shard_map/sc,sx->cx/dot_general | solution.py:34
  74.9 0.0 copy-start.2
  74.9 0.0 reduce-scatter.3.cloned.1.call-update
  74.9 0.7 copy-done.2
  75.6 1.6 stack.2
  77.2 15.6 %all-to-all-start = ((bf16[64,512,32]{1,2,0:T(8,128)(2,1)}), bf16[64,512,32]{1,2,0:T(8,128)(2,1)S(1)}, u32[]{:S(2)}, u32[]{:S(2)}) async-start(bf16[64,512,32]{1,2,0:T(8,128)(2,1)} %stack.2), calls=%async_computation.1 | async-start | bytes 4194304 | tf_op jit(solution)/shard_map/all_to_all | solution.py:29
  92.8 0.0 reduce-scatter.5.cloned.1.call-start
  92.9 0.0 copy-done
  92.9 0.0 copy-done.1
  92.9 1.7 fusion.7
  94.6 141.6 %reduce-scatter.3.cloned.1.call-done = bf16[8,16384]{1,0:T(8,128)(2,1)} async-done(((bf16[128,16384]{1,0:T(8,128)(2,1)}), bf16[8,16384]{1,0:T(8,128)(2,1)}) %reduce-scatter.3.cloned.1.call-update) | async-done | bytes 262160 | tf_op jit(solution)/shard_map/reduce_scatter | solution.py:35
  236.3 1.0 copy.11
  237.3 0.2 copy.9
  237.5 0.0 all-to-all-done
  237.5 3.7 %convolution_add_fusion = f32[256,2048]{1,0:T(8,128)} fusion(f32[256,2048]{1,0:T(8,128)} %fusion.7, bf16[512,2048]{0,1:T(8,128)(2,1)S(1)} %bitcast.27, bf16[32,8,4,128]{3,2,1,0:T(4,128)(2,1)S(1)} %bitcast.29), kind=kOutput, calls=%fused_computation.1 | convolution fusion | flops 537395200 | bytes 6553600 | tf_op jit(solution)/shard_map/dot_general | solution.py:48
  241.1 0.0 reduce-scatter.5.cloned.1.call-update
  241.2 40.6 %reduce-scatter.5.cloned.1.call-done = f32[256,256]{1,0:T(8,128)} async-done(((f32[256,2048]{1,0:T(8,128)}), f32[256,256]{1,0:T(8,128)}) %reduce-scatter.5.cloned.1.call-update) | async-done | bytes 262160 | tf_op jit(solution)/shard_map/reduce_scatter | solution.py:50
  281.8 1.6 convert_element_type.8
  (4 shorter events, 0.0 us)
Async XLA Ops:
  6.5 86.3 %copy-start = (bf16[128,2048]{1,0:T(8,128)(2,1)S(1)}, bf16[128,2048]{1,0:T(8,128)(2,1)}, u32[]{:S(2)}) copy-start(bf16[128,2048]{1,0:T(8,128)(2,1)} %param.13) | copy-start | bytes 1572868
  6.5 5.0 %copy-start.3 = (s32[32]{0:T(128)S(1)}, s32[32]{0:T(128)}, u32[]{:S(2)}) copy-start(s32[32]{0:T(128)} %param.10) | copy-start | bytes 388
  6.5 5.0 %copy-start.4 = (s32[32]{0:T(128)S(1)}, s32[32]{0:T(128)}, u32[]{:S(2)}) copy-start(s32[32]{0:T(128)} %param.9) | copy-start | bytes 388
  6.5 5.0 %copy-start.5 = (s32[32,1]{0,1:T(1,128)S(1)}, s32[32,1]{0,1:T(1,128)}, u32[]{:S(2)}) copy-start(s32[32,1]{0,1:T(1,128)} %param.8) | copy-start | bytes 388
  6.5 62.8 %all-gather.2.cloned.1.call-start = ((), (), s32[]{:S(2)}) async-start(), calls=%async_computation.3 | async-start | bytes 5242880 | tf_op jit(solution)/shard_map/all_gather | solution.py:20
  9.5 226.7 %reduce-scatter.3.cloned.1.call-start = ((), (), s32[]{:S(2)}) async-start(), calls=%async_computation.4 | async-start | bytes 4456448 | tf_op jit(solution)/shard_map/reduce_scatter | solution.py:35
  74.9 0.8 copy-start.2
  77.2 15.6 %copy-start.1 = (bf16[256,128]{1,0:T(8,128)(2,1)S(1)}, bf16[256,128]{1,0:T(8,128)(2,1)}, u32[]{:S(2)}) copy-start(bf16[256,128]{1,0:T(8,128)(2,1)} %param.12) | copy-start | bytes 196612
  77.2 160.2 %all-to-all-start = ((bf16[64,512,32]{1,2,0:T(8,128)(2,1)}), bf16[64,512,32]{1,2,0:T(8,128)(2,1)S(1)}, u32[]{:S(2)}, u32[]{:S(2)}) async-start(bf16[64,512,32]{1,2,0:T(8,128)(2,1)} %stack.2), calls=%async_computation.1 | async-start | bytes 4194304 | tf_op jit(solution)/shard_map/all_to_all | solution.py:29
  92.8 189.0 %reduce-scatter.5.cloned.1.call-start = ((), (), s32[]{:S(2)}) async-start(), calls=%async_computation.5 | async-start | bytes 2359296 | tf_op jit(solution)/shard_map/reduce_scatter | solution.py:50
Sparse Core Ops, SparseCore 0:
  9.7 59.6 all-gather.1
  75.0 161.2 reduce-scatter.2
  241.3 40.4 reduce-scatter.4
